TPU v7x, 32 devices: a whole 2x2x4 slice. The times are simulated.
32 devices in a mesh: groups: 2 (over y), tm: 4 (over z), chan: 2 (over x), night: 2 (over core).
Axes of the slice: x: 2, y: 2, z: 4, core: 2. Of those that a mesh axis runs over, the one named last changes fastest.
Arguments:
- signal: bfloat16 [4, 1024, 8192], P(('groups', 'night'), 'tm', 'chan'), parts along dimension 0, may hold values from -6 to 6
- lengths: int32 [4], P(('groups', 'night')), parts along dimension 0, may hold values from 256 to 1024, as said below
- patch_weight: bfloat16 [256, 1024], replicated
- chan_embed: float32 [32, 1024], P('chan'), may hold values from -5 to 5
- ln_gain: float32 [1024], replicated, may hold values from 0.1 to 1.9
- qkv_weight: bfloat16 [3, 1024, 1024], P(None, None, 'chan'), may hold values from -0.1875 to 0.1875
- head_temp: float32 [16], P('chan'), may hold values from 0.8 to 3
- out_weight: bfloat16 [1024, 1024], P('chan'), may hold values from -0.1875 to 0.1875
Outputs:
- encoded: bfloat16 [4, 1024, 1024], P(('groups', 'night'), 'tm', 'chan'), parts along dimension 0
There are 2 independent parts, one for each index of `groups`. A program takes and returns all parts, laid end to end along the dimension named above; an argument that names none is the same for every part. Nothing has to cross between parts.
Inputs may be any that keep to these rules, and one draw needn't show every extreme that they name: `lengths`: each night's number of valid tokens; in every draw some night is complete (1024 tokens).
All inputs are finite; a program needn't handle non-finite values.
Results may differ from a plain program's by a relative error of at most 0.0037.
Values may be sent and summed in bfloat16 or wider, within the bound.
A program may use at most 64 MiB of HBM per device.

v0:
```python
import functools
import math

import jax
import jax.numpy as jnp
from jax import lax
from jax.experimental import pallas as pl
from jax.experimental.pallas import tpu as pltpu
from jax.sharding import PartitionSpec as P

CH = 32
HD = 64
WINDOW = 1024
LOADS = 4
CHUNKS = 8
SPLIT = 3
ITEMS = CHUNKS - SPLIT
LAG = 2
MESH = pl.DeviceIdType.MESH
GELU_A = math.sqrt(2.0 / math.pi)
GELU_B = GELU_A * 0.044715
LOG2E = math.log2(math.e)


def kernel(
    n, reach, far,
    lengths, temp, signal, patch_w, embed, gain, qkv_w, out_w,
    out,
    sig_v, pw_v, qkv_v, ow_v, part, send_p, recv_p, win, qz, acc, att, send_b, recv_b,
    load_sem, sig_sem, ps_sem, pr_sem, zs_sem, zr_sem, xs_sem, xr_sem, bs_sem, br_sem,
):
    me = lax.axis_index("tm")
    col = lax.axis_index("chan")
    other = 1 - col
    load_rows = sig_v.shape[1]
    tok = load_rows * LOADS
    rows = tok // CHUNKS
    per_load = CHUNKS // LOADS
    width = pw_v.shape[1]
    share = qkv_v.shape[2]
    heads = share // HD
    pairs = heads // 2
    patch = pw_v.shape[0]
    chans = embed.shape[0]
    f32, bf16 = jnp.float32, jnp.bfloat16

    def sig_copy(r):
        return pltpu.make_async_copy(
            signal.at[0, pl.ds(r * load_rows, load_rows), :], sig_v.at[r], sig_sem.at[r]
        )

    loads = [
        pltpu.make_async_copy(patch_w, pw_v, load_sem.at[0]),
        pltpu.make_async_copy(qkv_w, qkv_v, load_sem.at[1]),
        pltpu.make_async_copy(out_w, ow_v, load_sem.at[2]),
    ]
    barrier = pltpu.get_barrier_semaphore()
    pl.semaphore_signal(barrier, inc=1, device_id={"chan": other}, device_id_type=MESH)

    @pl.when(me > 0)
    def _():
        pl.semaphore_signal(barrier, inc=1, device_id={"tm": me - 1}, device_id_type=MESH)

    @pl.when(me < n - 1)
    def _():
        pl.semaphore_signal(barrier, inc=1, device_id={"tm": me + 1}, device_id_type=MESH)

    loads[0].start()
    for r in range(LOADS):
        sig_copy(r).start()
    loads[1].start()
    loads[2].start()

    def part_copy(r):
        return pltpu.make_async_remote_copy(
            src_ref=send_p.at[r], dst_ref=recv_p.at[r], send_sem=ps_sem.at[r],
            recv_sem=pr_sem.at[r], device_id={"chan": other}, device_id_type=MESH,
        )

    def slot_of(side, d):
        return 2 * (d - 1) + side + 1

    def source(side, d):
        return me - d if side == 0 else me + d

    def held(side, d):
        s = source(side, d)
        return (s >= 0) & (s < n)

    def sends(side, d):
        nxt = me + 1 if side == 0 else me - 1
        return held(side, d - 1) & (nxt >= 0) & (nxt < n)

    def row_of(j):
        return jnp.where(j < SPLIT, 2 * j + col, j + SPLIT)

    def z_copy(side, d, j):
        src = jnp.where(d == 1, 0, slot_of(side, d - 1))
        dst = slot_of(side, d)
        nxt = me + 1 if side == 0 else me - 1
        r = row_of(j)
        return pltpu.make_async_remote_copy(
            src_ref=win.at[src, r], dst_ref=win.at[dst, r], send_sem=zs_sem.at[dst, j],
            recv_sem=zr_sem.at[dst, j], device_id={"tm": nxt}, device_id_type=MESH,
        )

    def x_copy(slot, r, j):
        return pltpu.make_async_remote_copy(
            src_ref=win.at[slot, r], dst_ref=win.at[slot, r], send_sem=xs_sem.at[slot, j],
            recv_sem=xr_sem.at[slot, j], device_id={"chan": other}, device_id_type=MESH,
        )

    loads[0].wait()

    def patch_step(r):
        sig_copy(r).wait()
        half = width // 2

        def col_step(b, carry):
            cs = pl.ds(pl.multiple_of(b * half, half), half)
            w = pw_v[:, cs]
            total = jnp.zeros((load_rows, half), f32)
            for c0 in range(0, chans, 4):
                lhs = jnp.concatenate(
                    [sig_v[r, :, (c0 + c) * patch : (c0 + c + 1) * patch] for c in range(4)], axis=0
                )
                y4 = jnp.dot(lhs, w, preferred_element_type=f32)
                for c in range(4):
                    y = y4[c * load_rows : (c + 1) * load_rows] + embed[c0 + c : c0 + c + 1, cs]
                    t = jnp.tanh(y * (GELU_A + GELU_B * (y * y)))
                    total = total + (y + y * t)
            total = total * (0.5 / CH)
            for i in range(per_load):
                piece = total[i * rows : (i + 1) * rows]
                part[r * per_load + i, :, cs] = piece
                send_p[r * per_load + i, :, cs] = piece.astype(bf16)
            return carry

        lax.fori_loop(0, 2, col_step, 0)

        @pl.when(r == 0)
        def _():
            peers = 1 + jnp.where(me > 0, 1, 0) + jnp.where(me < n - 1, 1, 0)
            pl.semaphore_wait(barrier, peers)

        for i in range(per_load):
            part_copy(r * per_load + i).start()

    def norm_step(r):
        part_copy(r).wait_recv()
        pooled = part[r] + recv_p[r].astype(f32)
        part[r] = pooled
        center = pooled - jnp.mean(pooled, axis=-1, keepdims=True)
        spread = jnp.mean(center * center, axis=-1, keepdims=True)
        win[0, r] = (center * lax.rsqrt(spread + 1e-05) * gain[...]).astype(bf16)

        relay_out(r, 1)

    def handled(r):
        return (r >= 2 * SPLIT) | (lax.rem(r, 2) == col)

    def item_of(r):
        return jnp.where(r < 2 * SPLIT, r // 2, r - SPLIT)

    def relay_out(r, d):
        for side in range(2):
            @pl.when(handled(r) & sends(side, d))
            def _(side=side):
                z_copy(side, d, item_of(r)).start()

    def load_loop(r, carry):
        patch_step(r)
        return carry

    lax.fori_loop(0, LOADS, load_loop, 0)

    lane_block = lax.broadcasted_iota(jnp.int32, (256, 256), 0) // HD
    sub_block = lax.broadcasted_iota(jnp.int32, (256, 256), 1) // HD
    means = jnp.where(lane_block == sub_block, 1.0 / HD, 0.0).astype(bf16)
    low = lax.broadcasted_iota(jnp.int32, (tok, 2 * HD), 1) < HD

    def unit(x):
        outs = []
        for b in range(share // 256):
            y = x[:, b * 256 : (b + 1) * 256]
            ms = jnp.dot((y * y).astype(bf16), means, preferred_element_type=f32)
            outs.append((y * lax.rsqrt(ms + 1e-06)).astype(bf16))
        return jnp.concatenate(outs, axis=1)

    def project_queries():
        loads[1].wait()
        q = unit(jnp.dot(win[0].reshape(tok, width), qkv_v[0], preferred_element_type=f32))
        for p in range(pairs):
            qp = q[:, p * 2 * HD : (p + 1) * 2 * HD]
            zero = jnp.zeros_like(qp)
            qz[2 * p] = jnp.where(low, qp, zero)
            qz[2 * p + 1] = jnp.where(low, zero, qp)

    acc[...] = jnp.zeros_like(acc)
    valid_len = lengths[0]

    def attend(slot, src):
        x = win[slot].reshape(tok, width)
        k = unit(jnp.dot(x, qkv_v[1], preferred_element_type=f32))
        v = jnp.dot(x, qkv_v[2], preferred_element_type=f32)
        key_pos = src * tok + lax.broadcasted_iota(jnp.int32, (tok, 2 * HD), 0)
        ok = jnp.where(key_pos < valid_len, 1.0, 0.0)
        for p in range(pairs):
            kp = k[:, p * 2 * HD : (p + 1) * 2 * HD]
            vp = v[:, p * 2 * HD : (p + 1) * 2 * HD] * ok
            for h in range(2):
                rhs = jnp.where(low, vp, ok) if h == 0 else jnp.where(low, ok, vp)
                s = lax.dot_general(
                    qz[2 * p + h], kp, (((1,), (1,)), ((), ())), preferred_element_type=f32
                )
                e = jnp.exp2(s * (temp[2 * p + h] * (HD**-0.5 * LOG2E)))
                if far:
                    gap = (me - src) * tok + (
                        lax.broadcasted_iota(jnp.int32, (tok, tok), 0)
                        - lax.broadcasted_iota(jnp.int32, (tok, tok), 1)
                    )
                    e = jnp.where(jnp.abs(gap) <= WINDOW, e, 0.0)
                acc[2 * p + h] += jnp.dot(
                    e.astype(bf16), rhs.astype(bf16), preferred_element_type=f32
                )

    def relay(d, r):
        for side in range(2):
            @pl.when(handled(r) & held(side, d))
            def _(side=side):
                z_copy(side, d, item_of(r)).wait_recv()
                if d < reach:
                    @pl.when(sends(side, d + 1))
                    def _():
                        z_copy(side, d + 1, item_of(r)).start()

                @pl.when(r < 2 * SPLIT)
                def _():
                    x_copy(slot_of(side, d), r, item_of(r)).start()

    def attend_at(dist):
        def slot_step(i, c):
            src = jnp.where(i == 0, me - dist, me + dist)
            slot = jnp.where(dist == 0, 0, 2 * (dist - 1) + i + 1)

            @pl.when((src >= 0) & (src < n) & ((dist > 0) | (i == 0)))
            def _():
                @pl.when(dist > 0)
                def _():
                    for j in range(SPLIT):
                        x_copy(slot, 2 * j + other, j).wait_recv()

                attend(slot, src)

            return c

        lax.fori_loop(0, 2, slot_step, 0)

    def event(t, carry):
        @pl.when(t < CHUNKS)
        def _():
            norm_step(t)

        for d in range(1, reach + 1):
            r = t - LAG * d

            @pl.when((r >= 0) & (r < CHUNKS))
            def _(d=d, r=r):
                relay(d, r)

        late = t - CHUNKS + 1

        @pl.when((late >= 0) & (lax.rem(late, LAG) == 0))
        def _():
            @pl.when(late == 0)
            def _():
                project_queries()

            attend_at(late // LAG)

        return carry

    lax.fori_loop(0, CHUNKS + LAG * reach, event, 0)

    query_pos = me * tok + lax.broadcasted_iota(jnp.int32, (tok, 2 * HD), 0)
    live = query_pos < valid_len
    for p in range(pairs):
        a0, a1 = acc[2 * p], acc[2 * p + 1]
        num = jnp.where(low, a0, a1)
        den = pltpu.roll(jnp.where(low, a1, a0), HD, 1)
        den = jnp.where(live, den, 1.0)
        att[:, p * 2 * HD : (p + 1) * 2 * HD] = (num / den).astype(bf16)

    loads[2].wait()
    theirs = pl.ds(pl.multiple_of(other * share, share), share)
    mine = pl.ds(pl.multiple_of(col * share, share), share)

    def branch_copy(b):
        return pltpu.make_async_remote_copy(
            src_ref=send_b.at[b], dst_ref=recv_b.at[b], send_sem=bs_sem.at[b],
            recv_sem=br_sem.at[b], device_id={"chan": other}, device_id_type=MESH,
        )

    for b in range(2):
        a = att[b * (tok // 2) : (b + 1) * (tok // 2), :]
        send_b[b] = jnp.dot(a, ow_v[:, theirs], preferred_element_type=f32).astype(bf16)
        branch_copy(b).start()
    own = jnp.dot(att[...], ow_v[:, mine], preferred_element_type=f32)
    own = own + part[:, :, mine].reshape(tok, share)
    for b in range(2):
        rs = slice(b * (tok // 2), (b + 1) * (tok // 2))
        branch_copy(b).wait_recv()
        pos = me * tok + b * (tok // 2) + lax.broadcasted_iota(jnp.int32, (tok // 2, share), 0)
        total = own[rs] + recv_b[b].astype(f32)
        out[0, rs, :] = jnp.where(pos < valid_len, total, 0.0).astype(bf16)

    for r in range(CHUNKS):
        part_copy(r).wait_send()
    for b in range(2):
        branch_copy(b).wait_send()

    def drain(d, carry):
        for side in range(2):
            @pl.when(sends(side, d))
            def _(side=side):
                for j in range(ITEMS):
                    z_copy(side, d, j).wait_send()

            @pl.when(held(side, d))
            def _(side=side):
                for j in range(SPLIT):
                    x_copy(slot_of(side, d), 2 * j + col, j).wait_send()

        return carry

    lax.fori_loop(1, reach + 1, drain, 0)


def body(n, signal, lengths, patch_weight, chan_embed, ln_gain, qkv_weight, head_temp, out_weight):
    _, tok, samples = signal.shape
    rows = tok // CHUNKS
    patch, width = patch_weight.shape
    share = qkv_weight.shape[2]
    heads = head_temp.shape[0]
    full = WINDOW // tok
    reach = min(full, n - 1)
    slots = 2 * reach + 1
    f32, bf16 = jnp.float32, jnp.bfloat16
    vmem = pl.BlockSpec(memory_space=pltpu.VMEM)
    smem = pl.BlockSpec(memory_space=pltpu.SMEM)
    anyw = pl.BlockSpec(memory_space=pl.ANY)
    dma = pltpu.SemaphoreType.DMA
    return pl.pallas_call(
        functools.partial(kernel, n, reach, n - 1 >= full),
        out_shape=jax.ShapeDtypeStruct((1, tok, share), bf16),
        in_specs=[smem, smem, anyw, anyw, vmem, vmem, anyw, anyw],
        out_specs=vmem,
        scratch_shapes=[
            pltpu.VMEM((LOADS, tok // LOADS, samples), bf16),
            pltpu.VMEM((patch, width), bf16),
            pltpu.VMEM(qkv_weight.shape, bf16),
            pltpu.VMEM(out_weight.shape, bf16),
            pltpu.VMEM((CHUNKS, rows, width), f32),
            pltpu.VMEM((CHUNKS, rows, width), bf16),
            pltpu.VMEM((CHUNKS, rows, width), bf16),
            pltpu.VMEM((slots, CHUNKS, rows, width), bf16),
            pltpu.VMEM((heads, tok, 2 * HD), bf16),
            pltpu.VMEM((heads, tok, 2 * HD), f32),
            pltpu.VMEM((tok, share), bf16),
            pltpu.VMEM((2, tok // 2, share), bf16),
            pltpu.VMEM((2, tok // 2, share), bf16),
            dma((3,)),
            dma((LOADS,)),
            dma((CHUNKS,)),
            dma((CHUNKS,)),
            dma((slots, ITEMS)),
            dma((slots, ITEMS)),
            dma((slots, SPLIT)),
            dma((slots, SPLIT)),
            dma((2,)),
            dma((2,)),
        ],
        compiler_params=pltpu.CompilerParams(
            collective_id=0, has_side_effects=True, vmem_limit_bytes=56 * 1024 * 1024
        ),
    )(
        lengths, head_temp, signal, patch_weight, chan_embed, ln_gain.reshape(1, width),
        qkv_weight, out_weight,
    )


def solution(mesh):
    return jax.shard_map(
        functools.partial(body, mesh.shape["tm"]),
        mesh=mesh,
        in_specs=(
            P(("groups", "night"), "tm", "chan"),
            P(("groups", "night")),
            P(),
            P("chan", None),
            P(),
            P(None, None, "chan"),
            P("chan"),
            P("chan", None),
        ),
        out_specs=P(("groups", "night"), "tm", "chan"),
        check_vma=False,
    )
```

profile of v0, /device:TPU:0, one launch (start us, length us, event | category | flops | bytes accessed | tf_op | source)
XLA Modules:
  0.0 48.4 jit_solution(73214755297939749)
XLA Ops:
  0.7 46.1 %shard_map.82 = bf16[1,256,512]{2,1,0:T(8,128)(2,1)} custom-call(s32[1]{0:T(128)S(6)} %copy.10.lengths, f32[8]{0:T(128)} %temp.1, bf16[1,256,4096]{2,1,0:T(8,128)(2,1)} %signal.1, bf16[256,1024]{1,0:T(8,128)(2,1)} %patch_w.1, f32[16,1024]{1,0:T(8,128)} %embed.1, f32[1,1024]{1,0:T(1,128)} %bitcast.1, bf16[3,1024,512]{2,1,0:T(8,128)(2,1)} %qkv_w.1, ...), custom_call_target="tpu_custom_call" | custom-call | tf_op jit(solution)/shard_map/pallas_call | solution.py:353
  46.7 1.7 %copy.11 = bf16[1,256,512]{2,1,0:T(8,128)(2,1)} copy(bf16[1,256,512]{2,1,0:T(8,128)(2,1)} %shard_map.82) | data formatting | bytes 524288
where the time goes:
time: 48.6 us; the launch traced here: 48.4 us
  Pallas kernels  46.1 us (95%)
  local copies, waits for them, and re-layouts  1.67 us (3%)
  between operations  0.66 us (1%)
    pallas_call x1, Pallas kernels, body(): pl.pallas_call(functools.partial(kernel, n, reach, n - 1 >= full), out_sh...  46.1 us
    unnamed x1, local copies, waits for them, and re-layouts  1.67 us

commit v1 on v0

--- a/solution.py
+++ b/solution.py
@@ -336,6 +336,328 @@
     lax.fori_loop(1, reach + 1, drain, 0)
 
 
+GRAIN = 8
+PIECES = ((0, 1), (1, 2), (2, 4), (4, 6), (6, 8))
+DELAY = 3
+
+
+def split_kernel(
+    n,
+    lengths, temp, signal, patch_w, embed, gain, qkv_w, out_w,
+    out,
+    sig_v, pw_v, qkv_v, ow_v, part, send_p, recv_p, normed, send_z, recv_z, qz, rhs, acc,
+    send_a, recv_a, own_v, send_b, recv_b,
+    load_sem, sig_sem, ps_sem, pr_sem, zs_sem, zr_sem, as_sem, ar_sem, bs_sem, br_sem,
+):
+    me = lax.axis_index("tm")
+    col = lax.axis_index("chan")
+    other = 1 - col
+    rows = sig_v.shape[1]
+    tok = rows * GRAIN
+    width = pw_v.shape[1]
+    share = qkv_v.shape[2]
+    patch = pw_v.shape[0]
+    chans = embed.shape[0]
+    blocks = recv_z.shape[0]
+    size = tok // blocks
+    per_block = GRAIN // blocks
+    pair = 2 * HD
+    f32, bf16 = jnp.float32, jnp.bfloat16
+
+    def sig_copy(r):
+        return pltpu.make_async_copy(
+            signal.at[0, pl.ds(r * rows, rows), :], sig_v.at[r], sig_sem.at[r]
+        )
+
+    loads = [
+        pltpu.make_async_copy(patch_w, pw_v, load_sem.at[0]),
+        pltpu.make_async_copy(qkv_w, qkv_v, load_sem.at[1]),
+        pltpu.make_async_copy(out_w, ow_v, load_sem.at[2]),
+    ]
+    barrier = pltpu.get_barrier_semaphore()
+    pl.semaphore_signal(barrier, inc=1, device_id={"chan": other}, device_id_type=MESH)
+    for k in range(1, n):
+        pl.semaphore_signal(
+            barrier, inc=1, device_id={"tm": lax.rem(me + k, n)}, device_id_type=MESH
+        )
+    loads[0].start()
+    for r in range(GRAIN):
+        sig_copy(r).start()
+    loads[1].start()
+    loads[2].start()
+
+    def part_copy(r):
+        return pltpu.make_async_remote_copy(
+            src_ref=send_p.at[r], dst_ref=recv_p.at[r], send_sem=ps_sem.at[r],
+            recv_sem=pr_sem.at[r], device_id={"chan": other}, device_id_type=MESH,
+        )
+
+    def span(p):
+        b, g = PIECES[p][0] // per_block, PIECES[p][0] % per_block
+        return b, pl.ds(g * rows, (PIECES[p][1] - PIECES[p][0]) * rows)
+
+    def z_send(p, dest):
+        b, rs = span(p)
+        return pltpu.make_async_remote_copy(
+            src_ref=send_z.at[b, dest, :, rs], dst_ref=recv_z.at[b, :, me, rs],
+            send_sem=zs_sem.at[p, dest], recv_sem=zr_sem.at[p, me],
+            device_id={"tm": dest}, device_id_type=MESH,
+        )
+
+    def z_recv(p, src):
+        b, rs = span(p)
+        return pltpu.make_async_remote_copy(
+            src_ref=send_z.at[b, src, :, rs], dst_ref=recv_z.at[b, :, src, rs],
+            send_sem=zs_sem.at[p, src], recv_sem=zr_sem.at[p, src],
+            device_id={"tm": src}, device_id_type=MESH,
+        )
+
+    def a_send(i, dest):
+        return pltpu.make_async_remote_copy(
+            src_ref=send_a.at[i, dest], dst_ref=recv_a.at[i, me], send_sem=as_sem.at[i, dest],
+            recv_sem=ar_sem.at[i, me], device_id={"tm": dest}, device_id_type=MESH,
+        )
+
+    def a_recv(i, src):
+        return pltpu.make_async_remote_copy(
+            src_ref=send_a.at[i, src], dst_ref=recv_a.at[i, src], send_sem=as_sem.at[i, src],
+            recv_sem=ar_sem.at[i, src], device_id={"tm": src}, device_id_type=MESH,
+        )
+
+    def b_copy(i):
+        return pltpu.make_async_remote_copy(
+            src_ref=send_b.at[i], dst_ref=recv_b.at[i], send_sem=bs_sem.at[i],
+            recv_sem=br_sem.at[i], device_id={"chan": other}, device_id_type=MESH,
+        )
+
+    others = [lax.rem(me + k, n) for k in range(1, n)]
+    loads[0].wait()
+    group = 256 // rows
+
+    def patch_step(r):
+        sig_copy(r).wait()
+        half = width // 2
+
+        def col_step(b, carry):
+            cs = pl.ds(pl.multiple_of(b * half, half), half)
+            w = pw_v[:, cs]
+            total = jnp.zeros((rows, half), f32)
+            for c0 in range(0, chans, group):
+                lhs = jnp.concatenate(
+                    [sig_v[r, :, (c0 + c) * patch : (c0 + c + 1) * patch] for c in range(group)],
+                    axis=0,
+                )
+                ys = jnp.dot(lhs, w, preferred_element_type=f32)
+                for c in range(group):
+                    y = ys[c * rows : (c + 1) * rows] + embed[c0 + c : c0 + c + 1, cs]
+                    t = jnp.tanh(y * (GELU_A + GELU_B * (y * y)))
+                    total = total + (y + y * t)
+            total = total * (0.5 / CH)
+            part[r, :, cs] = total
+            send_p[r, :, cs] = total.astype(bf16)
+            return carry
+
+        lax.fori_loop(0, 2, col_step, 0)
+
+        @pl.when(r == 0)
+        def _():
+            pl.semaphore_wait(barrier, n)
+
+        part_copy(r).start()
+
+    def norm_step(r):
+        part_copy(r).wait_recv()
+        pooled = part[r] + recv_p[r].astype(f32)
+        part[r] = pooled
+        center = pooled - jnp.mean(pooled, axis=-1, keepdims=True)
+        spread = jnp.mean(center * center, axis=-1, keepdims=True)
+        normed[r] = (center * lax.rsqrt(spread + 1e-05) * gain[...]).astype(bf16)
+
+    lane_block = lax.broadcasted_iota(jnp.int32, (256, 256), 0) // HD
+    sub_block = lax.broadcasted_iota(jnp.int32, (256, 256), 1) // HD
+    means = jnp.where(lane_block == sub_block, 1.0 / HD, 0.0).astype(bf16)
+
+    def unit(x):
+        outs = []
+        for b in range(share // 256):
+            y = x[:, b * 256 : (b + 1) * 256]
+            ms = jnp.dot((y * y).astype(bf16), means, preferred_element_type=f32)
+            outs.append((y * lax.rsqrt(ms + 1e-06)).astype(bf16))
+        return jnp.concatenate(outs, axis=1)
+
+    def project(p):
+        lo, hi = PIECES[p]
+        b, rs = span(p)
+        if p == 0:
+            loads[1].wait()
+        x = normed[lo:hi].reshape((hi - lo) * rows, width)
+        for i in range(3):
+            y = jnp.dot(x, qkv_v[i], preferred_element_type=f32)
+            y = unit(y) if i < 2 else y.astype(bf16)
+            for g in range(n):
+                send_z[b, g, i, rs] = y[:, g * pair : (g + 1) * pair]
+        for dest in others:
+            z_send(p, dest).start()
+        recv_z[b, :, me, rs] = send_z[b, me, :, rs]
+
+    def front(t, carry):
+        @pl.when(t < GRAIN)
+        def _():
+            patch_step(t)
+
+        @pl.when(t >= DELAY)
+        def _():
+            norm_step(t - DELAY)
+
+        for p in range(len(PIECES)):
+            @pl.when(t - DELAY == PIECES[p][1] - 1)
+            def _(p=p):
+                project(p)
+
+        return carry
+
+    lax.fori_loop(0, GRAIN + DELAY, front, 0)
+
+    count = n * size
+    valid_len = lengths[0]
+    low = lax.broadcasted_iota(jnp.int32, (count, pair), 1) < HD
+    local = lax.broadcasted_iota(jnp.int32, (count, pair), 0)
+    place = (local // size) * tok + local % size
+
+    def arrive(b):
+        for p in range(len(PIECES)):
+            if PIECES[p][0] // per_block == b:
+                for src in others:
+                    z_recv(p, src).wait_recv()
+        q = recv_z[b, 0].reshape(count, pair)
+        v = recv_z[b, 2].reshape(count, pair)
+        ok = jnp.where(place + b * size < valid_len, 1.0, 0.0)
+        v = v.astype(f32) * ok
+        zero = jnp.zeros_like(q)
+        qz[0, b] = jnp.where(low, q, zero)
+        qz[1, b] = jnp.where(low, zero, q)
+        rhs[0, b] = jnp.where(low, v, ok).astype(bf16)
+        rhs[1, b] = jnp.where(low, ok, v).astype(bf16)
+
+    scales = [temp[2 * me + h] * (HD**-0.5 * LOG2E) for h in range(2)]
+
+    def attend(i, k0, k1, first):
+        keys = recv_z[k0:k1, 1].reshape((k1 - k0) * count, pair)
+        for h in range(2):
+            s = lax.dot_general(
+                qz[h, i], keys, (((1,), (1,)), ((), ())), preferred_element_type=f32
+            )
+            e = jnp.exp2(s * scales[h]).astype(bf16)
+            o = jnp.dot(
+                e, rhs[h, k0:k1].reshape((k1 - k0) * count, pair), preferred_element_type=f32
+            )
+            if first:
+                acc[h, i] = o
+            else:
+                acc[h, i] += o
+
+    def finish(i):
+        a0, a1 = acc[0, i], acc[1, i]
+        num = jnp.where(low, a0, a1)
+        den = pltpu.roll(jnp.where(low, a1, a0), HD, 1)
+        den = jnp.where(place + i * size < valid_len, den, 1.0)
+        send_a[i] = (num / den).astype(bf16).reshape(n, size, pair)
+        for dest in others:
+            a_send(i, dest).start()
+        recv_a[i, me] = send_a[i, me]
+
+    for b in range(blocks):
+        arrive(b)
+        for i in range(b):
+            attend(i, b, b + 1, False)
+            if b == blocks - 1:
+                finish(i)
+        attend(b, 0, b + 1, True)
+    finish(blocks - 1)
+
+    loads[2].wait()
+    theirs = pl.ds(pl.multiple_of(other * share, share), share)
+    mine = pl.ds(pl.multiple_of(col * share, share), share)
+    for i in range(blocks):
+        for src in others:
+            a_recv(i, src).wait_recv()
+        a = jnp.concatenate([recv_a[i, g] for g in range(n)], axis=1)
+        send_b[i] = jnp.dot(a, ow_v[:, theirs], preferred_element_type=f32).astype(bf16)
+        b_copy(i).start()
+        own = jnp.dot(a, ow_v[:, mine], preferred_element_type=f32)
+        pooled = part[i * per_block : (i + 1) * per_block, :, mine].reshape(size, share)
+        own_v[i] = own + pooled
+    for i in range(blocks):
+        b_copy(i).wait_recv()
+        pos = me * tok + i * size + lax.broadcasted_iota(jnp.int32, (size, share), 0)
+        total = own_v[i] + recv_b[i].astype(f32)
+        out[0, i * size : (i + 1) * size, :] = jnp.where(pos < valid_len, total, 0.0).astype(bf16)
+
+    for r in range(GRAIN):
+        part_copy(r).wait_send()
+    for dest in others:
+        for p in range(len(PIECES)):
+            z_send(p, dest).wait_send()
+        for i in range(blocks):
+            a_send(i, dest).wait_send()
+    for i in range(blocks):
+        b_copy(i).wait_send()
+
+
+def split_body(n, lengths, head_temp, signal, patch_weight, chan_embed, gain, qkv_weight, out_weight):
+    _, tok, samples = signal.shape
+    rows = tok // GRAIN
+    patch, width = patch_weight.shape
+    share = qkv_weight.shape[2]
+    blocks = 4
+    size = tok // blocks
+    pair = 2 * HD
+    f32, bf16 = jnp.float32, jnp.bfloat16
+    vmem = pl.BlockSpec(memory_space=pltpu.VMEM)
+    smem = pl.BlockSpec(memory_space=pltpu.SMEM)
+    anyw = pl.BlockSpec(memory_space=pl.ANY)
+    dma = pltpu.SemaphoreType.DMA
+    return pl.pallas_call(
+        functools.partial(split_kernel, n),
+        out_shape=jax.ShapeDtypeStruct((1, tok, share), bf16),
+        in_specs=[smem, smem, anyw, anyw, vmem, vmem, anyw, anyw],
+        out_specs=vmem,
+        scratch_shapes=[
+            pltpu.VMEM((GRAIN, rows, samples), bf16),
+            pltpu.VMEM((patch, width), bf16),
+            pltpu.VMEM(qkv_weight.shape, bf16),
+            pltpu.VMEM(out_weight.shape, bf16),
+            pltpu.VMEM((GRAIN, rows, width), f32),
+            pltpu.VMEM((GRAIN, rows, width), bf16),
+            pltpu.VMEM((GRAIN, rows, width), bf16),
+            pltpu.VMEM((GRAIN, rows, width), bf16),
+            pltpu.VMEM((blocks, n, 3, size, pair), bf16),
+            pltpu.VMEM((blocks, 3, n, size, pair), bf16),
+            pltpu.VMEM((2, blocks, n * size, pair), bf16),
+            pltpu.VMEM((2, blocks, n * size, pair), bf16),
+            pltpu.VMEM((2, blocks, n * size, pair), f32),
+            pltpu.VMEM((blocks, n, size, pair), bf16),
+            pltpu.VMEM((blocks, n, size, pair), bf16),
+            pltpu.VMEM((blocks, size, share), f32),
+            pltpu.VMEM((blocks, size, share), bf16),
+            pltpu.VMEM((blocks, size, share), bf16),
+            dma((3,)),
+            dma((GRAIN,)),
+            dma((GRAIN,)),
+            dma((GRAIN,)),
+            dma((len(PIECES), n)),
+            dma((len(PIECES), n)),
+            dma((blocks, n)),
+            dma((blocks, n)),
+            dma((blocks,)),
+            dma((blocks,)),
+        ],
+        compiler_params=pltpu.CompilerParams(
+            collective_id=1, has_side_effects=True, vmem_limit_bytes=56 * 1024 * 1024
+        ),
+    )(lengths, head_temp, signal, patch_weight, chan_embed, gain, qkv_weight, out_weight)
+
+
 def body(n, signal, lengths, patch_weight, chan_embed, ln_gain, qkv_weight, head_temp, out_weight):
     _, tok, samples = signal.shape
     rows = tok // CHUNKS
@@ -350,6 +672,11 @@
     smem = pl.BlockSpec(memory_space=pltpu.SMEM)
     anyw = pl.BlockSpec(memory_space=pl.ANY)
     dma = pltpu.SemaphoreType.DMA
+    if n > 1 and n * tok <= WINDOW + 1 and heads == 2 * n and tok % 256 == 0:
+        return split_body(
+            n, lengths, head_temp, signal, patch_weight, chan_embed, ln_gain.reshape(1, width),
+            qkv_weight, out_weight,
+        )
     return pl.pallas_call(
         functools.partial(kernel, n, reach, n - 1 >= full),
         out_shape=jax.ShapeDtypeStruct((1, tok, share), bf16),

time: 48.6 us -> 44.8 us (0.922)
  Pallas kernels: 46.1 us -> 42.3 us
    pallas_call x1, Pallas kernels: 46.1 us -> 42.3 us  [split_body(): pl.pallas_call(functools.partial(split_kernel, n), out_shape=jax.ShapeDty...]
where the time goes in v1:
time: 44.8 us; the launch traced here: 44.6 us
  Pallas kernels  42.3 us (94%)
  local copies, waits for them, and re-layouts  1.67 us (4%)
  between operations  0.66 us (1%)
    pallas_call x1, Pallas kernels, split_body(): pl.pallas_call(functools.partial(split_kernel, n), out_shape=jax.ShapeDty...  42.3 us
    unnamed x1, local copies, waits for them, and re-layouts  1.67 us

profile of v1, /device:TPU:0, one launch (start us, length us, event | category | flops | bytes accessed | tf_op | source)
XLA Modules:
  0.0 44.6 jit_solution(1962265082204274450)
XLA Ops:
  0.7 42.3 %shard_map.82 = bf16[1,256,512]{2,1,0:T(8,128)(2,1)} custom-call(s32[1]{0:T(128)S(6)} %copy.10.lengths, f32[8]{0:T(128)} %temp.1, bf16[1,256,4096]{2,1,0:T(8,128)(2,1)} %signal.1, bf16[256,1024]{1,0:T(8,128)(2,1)} %patch_w.1, f32[16,1024]{1,0:T(8,128)} %embed.1, f32[1,1024]{1,0:T(1,128)} %bitcast.1, bf16[3,1024,512]{2,1,0:T(8,128)(2,1)} %qkv_w.1, ...), custom_call_target="tpu_custom_call" | custom-call | tf_op jit(solution)/shard_map/pallas_call | solution.py:620
  42.9 1.7 %copy.11 = bf16[1,256,512]{2,1,0:T(8,128)(2,1)} copy(bf16[1,256,512]{2,1,0:T(8,128)(2,1)} %shard_map.82) | data formatting | bytes 524288

commit v2 on v1

--- a/solution.py
+++ b/solution.py
@@ -339,13 +339,14 @@
 GRAIN = 8
 PIECES = ((0, 1), (1, 2), (2, 4), (4, 6), (6, 8))
 DELAY = 3
+AHEAD = 3
 
 
 def split_kernel(
     n,
-    lengths, temp, signal, patch_w, embed, gain, qkv_w, out_w,
+    lengths, temp, signal, patch_w, embed_w, gain_w, qkv_w, out_w,
     out,
-    sig_v, pw_v, qkv_v, ow_v, part, send_p, recv_p, normed, send_z, recv_z, qz, rhs, acc,
+    sig_v, pw_v, embed, gain, qkv_v, ow_v, part, send_p, recv_p, normed, send_z, recv_z, qz, rhs, acc,
     send_a, recv_a, own_v, send_b, recv_b,
     load_sem, sig_sem, ps_sem, pr_sem, zs_sem, zr_sem, as_sem, ar_sem, bs_sem, br_sem,
 ):
@@ -371,9 +372,14 @@
 
     loads = [
         pltpu.make_async_copy(patch_w, pw_v, load_sem.at[0]),
-        pltpu.make_async_copy(qkv_w, qkv_v, load_sem.at[1]),
-        pltpu.make_async_copy(out_w, ow_v, load_sem.at[2]),
+        pltpu.make_async_copy(out_w, ow_v, load_sem.at[1]),
+        pltpu.make_async_copy(embed_w, embed, load_sem.at[2]),
+        pltpu.make_async_copy(gain_w, gain, load_sem.at[3]),
     ]
+
+    def qkv_load(i):
+        return pltpu.make_async_copy(qkv_w.at[i], qkv_v.at[i], load_sem.at[4 + i])
+
     barrier = pltpu.get_barrier_semaphore()
     pl.semaphore_signal(barrier, inc=1, device_id={"chan": other}, device_id_type=MESH)
     for k in range(1, n):
@@ -381,10 +387,11 @@
             barrier, inc=1, device_id={"tm": lax.rem(me + k, n)}, device_id_type=MESH
         )
     loads[0].start()
-    for r in range(GRAIN):
+    sig_copy(0).start()
+    loads[2].start()
+    loads[3].start()
+    for r in range(1, AHEAD):
         sig_copy(r).start()
-    loads[1].start()
-    loads[2].start()
 
     def part_copy(r):
         return pltpu.make_async_remote_copy(
@@ -432,14 +439,29 @@
 
     others = [lax.rem(me + k, n) for k in range(1, n)]
     loads[0].wait()
+    loads[2].wait()
+    loads[3].wait()
     group = 256 // rows
 
     def patch_step(r):
         sig_copy(r).wait()
+
+        @pl.when(r + AHEAD < GRAIN)
+        def _():
+            sig_copy(r + AHEAD).start()
+
+        for i in range(3):
+            @pl.when(r == i)
+            def _(i=i):
+                qkv_load(i).start()
+
+        @pl.when(r == 3)
+        def _():
+            loads[1].start()
+
         half = width // 2
-
-        def col_step(b, carry):
-            cs = pl.ds(pl.multiple_of(b * half, half), half)
+        for b in range(2):
+            cs = slice(b * half, (b + 1) * half)
             w = pw_v[:, cs]
             total = jnp.zeros((rows, half), f32)
             for c0 in range(0, chans, group):
@@ -455,9 +477,6 @@
             total = total * (0.5 / CH)
             part[r, :, cs] = total
             send_p[r, :, cs] = total.astype(bf16)
-            return carry
-
-        lax.fori_loop(0, 2, col_step, 0)
 
         @pl.when(r == 0)
         def _():
@@ -488,10 +507,10 @@
     def project(p):
         lo, hi = PIECES[p]
         b, rs = span(p)
-        if p == 0:
-            loads[1].wait()
         x = normed[lo:hi].reshape((hi - lo) * rows, width)
         for i in range(3):
+            if p == 0:
+                qkv_load(i).wait()
             y = jnp.dot(x, qkv_v[i], preferred_element_type=f32)
             y = unit(y) if i < 2 else y.astype(bf16)
             for g in range(n):
@@ -575,7 +594,7 @@
         attend(b, 0, b + 1, True)
     finish(blocks - 1)
 
-    loads[2].wait()
+    loads[1].wait()
     theirs = pl.ds(pl.multiple_of(other * share, share), share)
     mine = pl.ds(pl.multiple_of(col * share, share), share)
     for i in range(blocks):
@@ -620,11 +639,13 @@
     return pl.pallas_call(
         functools.partial(split_kernel, n),
         out_shape=jax.ShapeDtypeStruct((1, tok, share), bf16),
-        in_specs=[smem, smem, anyw, anyw, vmem, vmem, anyw, anyw],
+        in_specs=[smem, smem, anyw, anyw, anyw, anyw, anyw, anyw],
         out_specs=vmem,
         scratch_shapes=[
             pltpu.VMEM((GRAIN, rows, samples), bf16),
             pltpu.VMEM((patch, width), bf16),
+            pltpu.VMEM(chan_embed.shape, f32),
+            pltpu.VMEM((1, width), f32),
             pltpu.VMEM(qkv_weight.shape, bf16),
             pltpu.VMEM(out_weight.shape, bf16),
             pltpu.VMEM((GRAIN, rows, width), f32),
@@ -641,7 +662,7 @@
             pltpu.VMEM((blocks, size, share), f32),
             pltpu.VMEM((blocks, size, share), bf16),
             pltpu.VMEM((blocks, size, share), bf16),
-            dma((3,)),
+            dma((7,)),
             dma((GRAIN,)),
             dma((GRAIN,)),
             dma((GRAIN,)),

time: 44.8 us -> 44 us (0.982)
  Pallas kernels: 42.3 us -> 41.5 us
    pallas_call x1, Pallas kernels: 42.3 us -> 41.5 us  [split_body(): pl.pallas_call(functools.partial(split_kernel, n), out_shape=jax.ShapeDty...]
where the time goes in v2:
time: 44 us; the launch traced here: 43.9 us
  Pallas kernels  41.5 us (94%)
  local copies, waits for them, and re-layouts  1.67 us (4%)
  between operations  0.66 us (2%)
    pallas_call x1, Pallas kernels, split_body(): pl.pallas_call(functools.partial(split_kernel, n), out_shape=jax.ShapeDty...  41.5 us
    unnamed x1, local copies, waits for them, and re-layouts  1.67 us

profile of v2, /device:TPU:0, one launch (start us, length us, event | category | flops | bytes accessed | tf_op | source)
XLA Modules:
  0.0 43.9 jit_solution(14130615290872234359)
XLA Ops:
  0.7 41.5 %shard_map.82 = bf16[1,256,512]{2,1,0:T(8,128)(2,1)} custom-call(s32[1]{0:T(128)S(6)} %copy.10.lengths, f32[8]{0:T(128)} %temp.1, bf16[1,256,4096]{2,1,0:T(8,128)(2,1)} %signal.1, bf16[256,1024]{1,0:T(8,128)(2,1)} %patch_w.1, f32[16,1024]{1,0:T(8,128)} %embed_w.1, f32[1,1024]{1,0:T(1,128)} %bitcast.1, bf16[3,1024,512]{2,1,0:T(8,128)(2,1)} %qkv_w.1, ...), custom_call_target="tpu_custom_call" | custom-call | tf_op jit(solution)/shard_map/pallas_call | solution.py:639
  42.2 1.7 %copy.11 = bf16[1,256,512]{2,1,0:T(8,128)(2,1)} copy(bf16[1,256,512]{2,1,0:T(8,128)(2,1)} %shard_map.82) | data formatting | bytes 524288
